TPU v7x, 32 devices: a whole 2x2x4 slice. The times are simulated.
32 devices in a mesh: fsdp: 4 (over y, x), ctx: 4 (over z), tp: 2 (over core).
Axes of the slice: x: 2, y: 2, z: 4, core: 2. Of those that a mesh axis runs over, the one named last changes fastest.
Arguments:
- tokens: bfloat16 [2, 2, 4, 128, 2304], P(None, None, 'ctx', 'fsdp'), may hold values from -6 to 6
- segments: int32 [2, 2, 4, 128], P(None, None, 'ctx', 'fsdp'), may hold values from 0 to 3, as said below
- stretch_order: int32 [4], replicated, may hold values from 0 to 3, as said below
- norm_gains: float32 [4, 2304], replicated, may hold values from 0.25 to 1.75
- query_proj: bfloat16 [2304, 2048], P('fsdp', 'tp'), may hold values from -0.125 to 0.125
- keyval_proj: bfloat16 [2304, 2, 1024], P('fsdp', None, 'tp'), may hold values from -0.125 to 0.125
- attn_proj: bfloat16 [2304, 2048], P('fsdp', 'tp'), may hold values from -0.125 to 0.125
- ffn_in: bfloat16 [2304, 2, 9216], P('fsdp', None, 'tp'), may hold values from -0.125 to 0.125
- ffn_out: bfloat16 [2304, 9216], P('fsdp', 'tp'), may hold values from -0.0625 to 0.0625
- cotangent: bfloat16 [2, 2, 4, 128, 2304], P(None, None, 'ctx', 'fsdp'), may hold values from -6 to 6
Outputs:
- result: bfloat16 [2, 2, 4, 128, 2304], P(None, None, 'ctx', 'fsdp')
- grad_tokens: float32 [2, 2, 4, 128, 2304], P(None, None, 'ctx', 'fsdp')
- grad_gains: float32 [4, 2304], replicated
- grad_query: float32 [2304, 2048], P('fsdp', 'tp')
- grad_keyval: float32 [2304, 2, 1024], P('fsdp', None, 'tp')
- grad_attn: float32 [2304, 2048], P('fsdp', 'tp')
- grad_ffn_in: float32 [2304, 2, 9216], P('fsdp', None, 'tp')
- grad_ffn_out: float32 [2304, 9216], P('fsdp', 'tp')
Inputs may be any that keep to these rules, and one draw needn't show every extreme that they name: `segments`: along the positions of a sequence the segment ids never fall; every sequence holds exactly four documents, ids 0 to 3. Each of 0 to 3 once; slot c holds position blocks stretch_order[c] and 7 - stretch_order[c] of every sequence.
All inputs are finite; a program needn't handle non-finite values.
Results may differ from a plain program's by a relative error of at most 0.015.
Values may be sent and summed in bfloat16 or wider, within the bound.
No kernel may reach another device: no remote copies, remote signals or barrier semaphores. Data moves between devices by JAX's collectives and lax.ppermute only.
A program may use at most 640 MiB of HBM per device.

v0:
```python
import jax
import jax.numpy as jnp
from jax import lax
from jax.sharding import PartitionSpec as P

HEAD_DIM = 256
SOFT_CAP = 50.0
NORM_EPS = 1e-06


def rms_factor(values):
    return lax.rsqrt(jnp.mean(values * values, axis=-1, keepdims=True) + NORM_EPS)


def norm_back(grad_out, values, scale_gain):
    factor = rms_factor(values)
    normed = values * factor
    grad_gain = jnp.sum(grad_out * normed, axis=0)
    scaled_grad = grad_out * scale_gain
    grad_in = factor * (
        scaled_grad - normed * jnp.mean(scaled_grad * normed, axis=-1, keepdims=True)
    )
    return (grad_in, grad_gain)


def gelu_parts(gate_vals):
    values, pullback = jax.vjp(lambda inputs: jax.nn.gelu(inputs, approximate=True), gate_vals)
    return (values, pullback(jnp.ones_like(gate_vals))[0])


def dot_nt(left, right):
    return lax.dot_general(
        left, right, (((1,), (1,)), ((), ())), preferred_element_type=jnp.float32
    )


def dot_tn(left, right):
    return lax.dot_general(
        left, right, (((0,), (0,)), ((), ())), preferred_element_type=jnp.float32
    )


def key_positions(first, span_len, local_rows, half_dev, ctx_count, half_stretch, stretch_order):
    index_vec = first + lax.iota(jnp.int32, span_len)
    device_pos = index_vec // local_rows
    fsdp_pos = device_pos // ctx_count
    ctx_pos = device_pos % ctx_count
    row_pos = index_vec % local_rows
    halves = row_pos // half_dev
    within = row_pos % half_dev
    slot_match = ctx_pos[:, None] == lax.iota(jnp.int32, ctx_count)[None, :]
    paired = jnp.sum(jnp.where(slot_match, stretch_order[None, :], 0), axis=1)
    placed = jnp.where(halves == 0, paired, 2 * ctx_count - 1 - paired)
    return placed * half_stretch + fsdp_pos * half_dev + within


def key_block_len(span_len, local_rows):
    unit_count = span_len // local_rows
    upper_units = max(1, 2048 // local_rows)
    chosen = 1
    for divisor in range(1, min(unit_count, upper_units) + 1):
        if unit_count % divisor == 0:
            chosen = divisor
    return chosen * local_rows


def body_scores(query_five, key_blk, query_pos, query_seg, key_pos, key_seg):
    raw_scores = jnp.einsum(
        "sqkge,sbke->skgqb", query_five, key_blk, preferred_element_type=jnp.float32
    ) * HEAD_DIM ** (-0.5)
    capped = SOFT_CAP * jnp.tanh(raw_scores / SOFT_CAP)
    allowed = (query_seg[:, :, None] == key_seg[:, None, :]) & (
        key_pos[None, None, :] <= query_pos[None, :, None]
    )
    return (capped, allowed[:, None, None])


def on_device(
    tokens,
    segments,
    stretch_order,
    norm_gains,
    query_proj,
    keyval_proj,
    attn_proj,
    ffn_in,
    ffn_out,
    cotangent,
):
    f32 = jnp.float32
    bf16 = jnp.bfloat16
    seq_count = tokens.shape[0]
    half_dev = tokens.shape[3]
    model_width = tokens.shape[4]
    local_rows = 2 * half_dev
    row_count = seq_count * local_rows
    fsdp_count = lax.axis_size("fsdp")
    ctx_count = lax.axis_size("ctx")
    half_stretch = half_dev * fsdp_count
    gain_pre, gain_post, gain_ffn, gain_last = (
        norm_gains[0],
        norm_gains[1],
        norm_gains[2],
        norm_gains[3],
    )
    tok_in = tokens.reshape(row_count, model_width).astype(f32)
    seg_local = segments.reshape(seq_count, local_rows)
    own_first = (lax.axis_index("fsdp") * ctx_count + lax.axis_index("ctx")) * local_rows
    own_pos = key_positions(
        own_first, local_rows, local_rows, half_dev, ctx_count, half_stretch, stretch_order
    )
    xnorm = (tok_in * rms_factor(tok_in) * gain_pre).astype(bf16)
    full_query, full_keyval, full_attn = (
        lax.all_gather(query_proj, "fsdp", axis=0, tiled=True),
        lax.all_gather(keyval_proj, "fsdp", axis=0, tiled=True),
        lax.all_gather(attn_proj, "fsdp", axis=0, tiled=True),
    )
    qcols = full_query.shape[1]
    kcols = full_keyval.shape[2]
    kv_local = kcols // HEAD_DIM
    group = qcols // HEAD_DIM // kv_local
    keyval_flat_w = full_keyval.reshape(model_width, 2 * kcols)
    query = jnp.dot(xnorm, full_query, preferred_element_type=f32).astype(bf16)
    keyval = jnp.dot(xnorm, keyval_flat_w, preferred_element_type=f32).astype(bf16)
    query_five = query.reshape(seq_count, local_rows, kv_local, group, HEAD_DIM)
    keyval_four = keyval.reshape(seq_count, local_rows, 2, kcols)
    kv_first, seg_first = (
        lax.all_gather(keyval_four, ("fsdp", "ctx"), axis=1, tiled=True),
        lax.all_gather(seg_local, ("fsdp", "ctx"), axis=1, tiled=True),
    )
    fwd_total = kv_first.shape[1]
    fwd_len = key_block_len(fwd_total, local_rows)

    def fwd_step(step_index, partial_sums):
        denom, mixture = partial_sums
        offset = step_index * fwd_len
        kv_blk = lax.dynamic_slice_in_dim(kv_first, offset, fwd_len, 1)
        seg_blk = lax.dynamic_slice_in_dim(seg_first, offset, fwd_len, 1)
        pos_blk = key_positions(
            offset, fwd_len, local_rows, half_dev, ctx_count, half_stretch, stretch_order
        )
        keys_blk = kv_blk[:, :, 0].reshape(seq_count, fwd_len, kv_local, HEAD_DIM)
        vals_blk = kv_blk[:, :, 1].reshape(seq_count, fwd_len, kv_local, HEAD_DIM)
        capped, allowed = body_scores(query_five, keys_blk, own_pos, seg_local, pos_blk, seg_blk)
        expo = jnp.where(allowed, jnp.exp(capped), 0.0)
        denom = denom + jnp.sum(expo, axis=-1)
        mixture = mixture + jnp.einsum(
            "skgqb,sbke->sqkge", expo.astype(bf16), vals_blk, preferred_element_type=f32
        )
        return (denom, mixture)

    start_fold = (
        jnp.zeros((seq_count, kv_local, group, local_rows), f32),
        jnp.zeros((seq_count, local_rows, kv_local, group, HEAD_DIM), f32),
    )
    denom, mixture = lax.fori_loop(0, fwd_total // fwd_len, fwd_step, start_fold)
    attended_five = (mixture / jnp.transpose(denom, (0, 3, 1, 2))[..., None]).astype(bf16)
    lse_local = jnp.log(denom)
    attended = attended_five.reshape(row_count, qcols)
    branch = lax.psum(dot_nt(attended, full_attn), "tp")
    hidden = tok_in + branch * rms_factor(branch) * gain_post
    hnorm = (hidden * rms_factor(hidden) * gain_ffn).astype(bf16)
    full_in, full_out = (
        lax.all_gather(ffn_in, "fsdp", axis=0, tiled=True),
        lax.all_gather(ffn_out, "fsdp", axis=0, tiled=True),
    )
    ff_local = full_out.shape[1]
    both = jnp.dot(
        hnorm, full_in.reshape(model_width, 2 * ff_local), preferred_element_type=f32
    ).reshape(row_count, 2, ff_local)
    gelu_vals, gelu_slope = gelu_parts(both[:, 0])
    middle = (gelu_vals * both[:, 1]).astype(bf16)
    ffout = lax.psum(dot_nt(middle, full_out), "tp")
    result = (hidden + ffout * rms_factor(ffout) * gain_last).astype(bf16)
    cot_in = cotangent.reshape(row_count, model_width).astype(f32)
    grad_ff, grad_last_gain = norm_back(cot_in, ffout, gain_last)
    grad_ffb = grad_ff.astype(bf16)
    back_in, back_out = (
        lax.all_gather(ffn_in, "fsdp", axis=0, tiled=True),
        lax.all_gather(ffn_out, "fsdp", axis=0, tiled=True),
    )
    grad_mid = jnp.dot(grad_ffb, back_out, preferred_element_type=f32)
    grad_both = (
        jnp.stack([grad_mid * both[:, 1] * gelu_slope, grad_mid * gelu_vals], axis=1)
        .astype(bf16)
        .reshape(row_count, 2 * ff_local)
    )
    grad_hn = lax.psum(dot_nt(grad_both, back_in.reshape(model_width, 2 * ff_local)), "tp")
    grad_hid_n, grad_ffn_gain = norm_back(grad_hn, hidden, gain_ffn)
    grad_hidden = cot_in + grad_hid_n
    grad_branch, grad_post_gain = norm_back(grad_hidden, branch, gain_post)
    grad_branchb = grad_branch.astype(bf16)
    grad_attended = jnp.dot(grad_branchb, full_attn, preferred_element_type=f32).astype(bf16)
    grad_att_five = grad_attended.reshape(seq_count, local_rows, kv_local, group, HEAD_DIM)
    delta = jnp.einsum("sqkge,sqkge->skgq", grad_att_five.astype(f32), attended_five.astype(f32))
    kv_all, seg_all = (kv_first, seg_first)
    total_keys = kv_all.shape[1]
    back_len = key_block_len(total_keys, local_rows)

    def back_step(step_index, partial_sums):
        grad_q_acc, kv_term = partial_sums
        offset = step_index * back_len
        kv_blk = lax.dynamic_slice_in_dim(kv_all, offset, back_len, 1)
        seg_blk = lax.dynamic_slice_in_dim(seg_all, offset, back_len, 1)
        pos_blk = key_positions(
            offset, back_len, local_rows, half_dev, ctx_count, half_stretch, stretch_order
        )
        keys_blk = kv_blk[:, :, 0].reshape(seq_count, back_len, kv_local, HEAD_DIM)
        vals_blk = kv_blk[:, :, 1].reshape(seq_count, back_len, kv_local, HEAD_DIM)
        capped, allowed = body_scores(query_five, keys_blk, own_pos, seg_local, pos_blk, seg_blk)
        prob = jnp.where(allowed, jnp.exp(capped - lse_local[..., None]), 0.0)
        grad_prob = jnp.einsum(
            "sqkge,sbke->skgqb", grad_att_five, vals_blk, preferred_element_type=f32
        )
        ratio = capped / SOFT_CAP
        grad_raw = (
            prob * (grad_prob - delta[..., None]) * (1.0 - ratio * ratio) * HEAD_DIM ** (-0.5)
        )
        raw_half = grad_raw.astype(bf16)
        prob_half = prob.astype(bf16)
        grad_q_acc = grad_q_acc + jnp.einsum(
            "skgqb,sbke->sqkge", raw_half, keys_blk, preferred_element_type=f32
        )
        grad_keys = jnp.einsum(
            "skgqb,sqkge->sbke", raw_half, query_five, preferred_element_type=f32
        )
        grad_vals = jnp.einsum(
            "skgqb,sqkge->sbke", prob_half, grad_att_five, preferred_element_type=f32
        )
        block_term = jnp.stack(
            [
                grad_keys.reshape(seq_count, back_len, kcols),
                grad_vals.reshape(seq_count, back_len, kcols),
            ],
            axis=2,
        )
        kv_term = lax.dynamic_update_slice_in_dim(kv_term, block_term, offset, 1)
        return (grad_q_acc, kv_term)

    start_back = (
        jnp.zeros((seq_count, local_rows, kv_local, group, HEAD_DIM), f32),
        jnp.zeros((seq_count, total_keys, 2, kcols), f32),
    )
    grad_q_acc, kv_term = lax.fori_loop(0, total_keys // back_len, back_step, start_back)
    grad_kv_own = lax.psum_scatter(kv_term, ("fsdp", "ctx"), scatter_dimension=1, tiled=True)
    grad_kv_rows = grad_kv_own.astype(bf16).reshape(row_count, 2 * kcols)
    grad_q_rows = grad_q_acc.astype(bf16).reshape(row_count, qcols)
    grad_xnorm = lax.psum(
        (dot_nt(grad_q_rows, full_query) + dot_nt(grad_kv_rows, keyval_flat_w)).astype(
            jnp.bfloat16
        ),
        "tp",
    ).astype(jnp.float32)
    grad_x_n, grad_pre_gain = norm_back(grad_xnorm, tok_in, gain_pre)
    grad_tokens = (grad_hidden + grad_x_n).reshape(tokens.shape)
    gain_stack = jnp.stack([grad_pre_gain, grad_post_gain, grad_ffn_gain, grad_last_gain], axis=0)
    grad_gains = lax.psum(gain_stack, ("fsdp", "ctx"))
    right_attn_in = jnp.concatenate([grad_q_rows, grad_kv_rows], axis=1)
    pairs_list = (
        (xnorm, right_attn_in),
        (grad_branchb, attended),
        (hnorm, grad_both),
        (grad_ffb, middle),
    )
    columns_list = []
    for left_side, right_side in pairs_list:
        columns_list.append(dot_tn(left_side, right_side))
    summed = lax.psum_scatter(
        jnp.concatenate(columns_list, axis=1), "fsdp", scatter_dimension=0, tiled=True
    )
    summed = lax.psum(summed, "ctx")
    own_width = summed.shape[0]
    edge_two = qcols + 2 * kcols
    edge_three = edge_two + qcols
    edge_four = edge_three + 2 * ff_local
    grad_query = summed[:, :qcols]
    grad_keyval = summed[:, qcols:edge_two].reshape(own_width, 2, kcols)
    grad_attn = summed[:, edge_two:edge_three]
    grad_ffn_in = summed[:, edge_three:edge_four].reshape(own_width, 2, ff_local)
    grad_ffn_out = summed[:, edge_four:]
    return (
        result.reshape(tokens.shape),
        grad_tokens,
        grad_gains,
        grad_query,
        grad_keyval,
        grad_attn,
        grad_ffn_in,
        grad_ffn_out,
    )


def solution(mesh):
    placed = (
        P(None, None, "ctx", "fsdp", None),
        P(None, None, "ctx", "fsdp"),
        P(),
        P(),
        P("fsdp", "tp"),
        P("fsdp", None, "tp"),
        P("fsdp", "tp"),
        P("fsdp", None, "tp"),
        P("fsdp", "tp"),
        P(None, None, "ctx", "fsdp", None),
    )
    return jax.shard_map(
        on_device,
        mesh=mesh,
        in_specs=placed,
        out_specs=(
            P(None, None, "ctx", "fsdp", None),
            P(None, None, "ctx", "fsdp", None),
            P(),
            P("fsdp", "tp"),
            P("fsdp", None, "tp"),
            P("fsdp", "tp"),
            P("fsdp", None, "tp"),
            P("fsdp", "tp"),
        ),
        check_vma=False,
    )
```

profile of v0, /device:TPU:0, one launch (start us, length us, event | category | flops | bytes accessed | tf_op | source)
XLA Modules:
  0.0 3955.3 jit_solution(13872691908073583657)
XLA Ops:
  9.8 59.8 %all-gather.8.cloned.1.call-done = bf16[2304,2,512]{2,1,0:T(2,128)(2,1)} async-done(((bf16[576,2,512]{2,1,0:T(2,128)(2,1)}), bf16[2304,2,512]{2,1,0:T(2,128)(2,1)}) %all-gather.8.cloned.1.call-update) | async-done | bytes 4718608 | tf_op jit(solution)/shard_map/all_gather | solution.py:115
  79.6 39.8 %all-gather = s32[16,64,2]{1,2,0:T(2,128)S(1)} all-gather(s32[1,64,2]{1,2,0:T(2,128)S(1)} %bitcast.200), channel_id=1, replica_groups=mesh['fsdp'=4,'ctx'=4,'tp'=2] {'fsdp','ctx'}, dimensions={0}, use_global_device_ids=true | all-gather | bytes 8704 | tf_op jit(solution)/shard_map/all_gather | solution.py:129
  132.1 75.8 %all-gather.10.cloned.1.call-done = bf16[2,1024,2,512]{3,2,0,1:T(2,128)(2,1)} async-done(((bf16[2,64,2,512]{3,2,0,1:T(2,128)(2,1)}), bf16[2,1024,2,512]{3,2,0,1:T(2,128)(2,1)}) %all-gather.10.cloned.1.call-update) | async-done | bytes 4194320 | tf_op jit(solution)/shard_map/all_gather | solution.py:128
  244.2 21.1 all-gather.14.cloned.1.call-done
  293.4 372.8 %all-gather.16.cloned.1.call-done = bf16[2304,2,4608]{2,0,1:T(8,128)(2,1)} async-done(((bf16[576,2,4608]{2,0,1:T(8,128)(2,1)}), bf16[2304,2,4608]{2,0,1:T(8,128)(2,1)}) %all-gather.16.cloned.1.call-update) | async-done | bytes 42467344 | tf_op jit(solution)/shard_map/all_gather | solution.py:164
  666.2 51.5 %copy.80 = bf16[2304,2,4608]{0,2,1:T(8,128)(2,1)} copy(bf16[2304,2,4608]{2,0,1:T(8,128)(2,1)} %all-gather.16.cloned.1.call-done) | data formatting | bytes 84934656 | tf_op jit(solution)/shard_map/all_gather | solution.py:164
  717.8 21.7 fusion
  742.6 121.0 %all-gather.18.cloned.1.call-done = bf16[2304,4608]{1,0:T(8,128)(2,1)} async-done(((bf16[576,4608]{1,0:T(8,128)(2,1)}), bf16[2304,4608]{1,0:T(8,128)(2,1)}) %all-gather.18.cloned.1.call-update) | async-done | bytes 21233680 | tf_op jit(solution)/shard_map/all_gather | solution.py:165
  863.6 12.0 fusion.88
  875.9 19.7 all-reduce.8.cloned.1.call-done
  902.1 12.5 fusion.10
  915.7 20.7 convolution_bitcast_fusion
  938.0 19.6 all-reduce.10.cloned.1.call-done
  1010.4 11.8 reshape.420
  1030.7 16.6 fusion.91
  1047.4 31.6 fusion.84
  1086.7 119.2 %reduce-scatter.8.cloned.1.call-done = f32[64,2048]{1,0:T(8,128)} async-done(((f32[1024,2048]{1,0:T(8,128)}), f32[64,2048]{1,0:T(8,128)}) %reduce-scatter.8.cloned.1.call-update) | async-done | bytes 524304
  1215.6 99.1 %pad_maximum_fusion = f32[2304,16896]{1,0:T(8,128)} fusion(f32[2304,4608]{1,0:T(8,128)} %fusion.91, f32[2304,9216]{1,0:T(8,128)} %fusion.84, f32[2304,1024]{1,0:T(8,128)} %fusion.90, f32[2304,2048]{1,0:T(8,128)} %fusion.52), kind=kLoop, calls=%fused_computation | loop fusion | flops 116785152 | bytes 311427072 | tf_op jit(solution)/shard_map/concatenate | solution.py:269
  1324.1 1259.3 %reduce-scatter.6.cloned.1.call-done = f32[576,16896]{1,0:T(8,128)} async-done(((f32[2304,16896]{1,0:T(8,128)}), f32[576,16896]{1,0:T(8,128)}) %reduce-scatter.6.cloned.1.call-update) | async-done | bytes 38928400 | tf_op jit(solution)/shard_map/reduce_scatter | solution.py:268
  2584.2 20.9 all-reduce.12.cloned.1.call-done
  2606.6 87.2 %psum.46 = f32[4,2304]{1,0:T(4,128)} all-reduce(f32[4,2304]{1,0:T(4,128)S(1)} %pad_maximum_fusion.2), channel_id=1, replica_groups=mesh['fsdp'=4,'ctx'=4,'tp'=2] {'fsdp','ctx'}, use_global_device_ids=true, to_apply=%region_20.21 | all-reduce | flops 9216 | bytes 73728 | tf_op jit(solution)/shard_map/psum | solution.py:257
  2696.3 1192.0 %all-reduce.14.cloned.1.call-done = f32[576,16896]{1,0:T(8,128)} async-done(((f32[576,16896]{1,0:T(8,128)}), f32[576,16896]{1,0:T(8,128)}) %all-reduce.14.cloned.1.call-update) | async-done | bytes 38928400 | tf_op jit(solution)/shard_map/psum | solution.py:271
  3897.8 15.0 slice.66
  3912.8 26.6 reshape.404
  (207 shorter events, 213.0 us)
Async XLA Ops:
  7.2 62.5 %all-gather.8.cloned.1.call-start = ((), (), s32[]{:S(2)}) async-start(), calls=%async_computation.2 | async-start | bytes 5898240 | tf_op jit(solution)/shard_map/all_gather | solution.py:115
  7.9 120.8 %all-gather.12.cloned.1.call-start = ((), (), s32[]{:S(2)}) async-start(), calls=%async_computation.4 | async-start | bytes 5898240 | tf_op jit(solution)/shard_map/all_gather | solution.py:114
  8.7 199.2 %all-gather.10.cloned.1.call-start = ((), (), s32[]{:S(2)}) async-start(), calls=%async_computation.3 | async-start | bytes 4456448 | tf_op jit(solution)/shard_map/all_gather | solution.py:128
  9.4 110.6 %copy-start.32 = (f32[2304]{0:T(1024)}, f32[2304]{0:T(1024)S(1)}, u32[]{:S(2)}) copy-start(f32[2304]{0:T(1024)S(1)} %get-tuple-element.119) | copy-start | bytes 27652
  9.4 282.3 %copy-start.34 = (f32[2304]{0:T(1024)}, f32[2304]{0:T(1024)S(1)}, u32[]{:S(2)}) copy-start(f32[2304]{0:T(1024)S(1)} %get-tuple-element.118) | copy-start | bytes 27652
  76.5 43.0 %copy-start.47 = (s32[4]{0:T(128)S(1)}, s32[4]{0:T(128)}, u32[]{:S(2)}) copy-start(s32[4]{0:T(128)} %param.12) | copy-start | bytes 52
  77.6 187.7 %all-gather.14.cloned.1.call-start = ((), (), s32[]{:S(2)}) async-start(), calls=%async_computation.5 | async-start | bytes 5898240 | tf_op jit(solution)/shard_map/all_gather | solution.py:116
  78.2 212.1 %all-reduce.6.cloned.1.call-start = ((), (), s32[]{:S(2)}) async-start(), calls=%async_computation.6 | async-start | bytes 2359296 | tf_op jit(solution)/shard_map/psum | solution.py:160
  78.3 53.5 %copy-start.41 = (f32[128]{0:T(128)}, f32[128]{0:T(128)S(1)}, u32[]{:S(2)}) copy-start(f32[128]{0:T(128)S(1)} %rsqrt.41) | copy-start | bytes 1540
  120.0 121.7 %copy-start.30 = (pred[2,64,1024]{2,1,0:T(8,128)(4,1)}, pred[2,64,1024]{2,1,0:T(8,128)(4,1)S(1)}, u32[]{:S(2)}) copy-start(pred[2,64,1024]{2,1,0:T(8,128)(4,1)S(1)} %compare_and_fusion) | copy-start | bytes 393220
  132.1 106.9 %copy-start.29 = (bf16[2,64,2,2,256]{4,3,2,1,0:T(2,128)(2,1)}, bf16[2,64,2,2,256]{4,3,2,1,0:T(2,128)(2,1)S(1)}, u32[]{:S(2)}) copy-start(bf16[2,64,2,2,256]{4,3,2,1,0:T(2,128)(2,1)S(1)} %reshape.393) | copy-start | bytes 786436
  244.2 26.1 copy-start.21
  270.3 395.9 %all-gather.16.cloned.1.call-start = ((), (), s32[]{:S(2)}) async-start(), calls=%async_computation.7 | async-start | bytes 53084160 | tf_op jit(solution)/shard_map/all_gather | solution.py:164
  280.6 583.0 %all-gather.18.cloned.1.call-start = ((), (), s32[]{:S(2)}) async-start(), calls=%async_computation.8 | async-start | bytes 26542080 | tf_op jit(solution)/shard_map/all_gather | solution.py:165
  281.4 614.3 %all-reduce.8.cloned.1.call-start = ((), (), s32[]{:S(2)}) async-start(), calls=%async_computation.9 | async-start | bytes 2359296 | tf_op jit(solution)/shard_map/psum | solution.py:173
  291.7 426.0 %copy-start.43 = (f32[128]{0:T(128)}, f32[128]{0:T(128)S(1)}, u32[]{:S(2)}) copy-start(f32[128]{0:T(128)S(1)} %add_rsqrt_fusion.3) | copy-start | bytes 1540
  875.7 81.9 %all-reduce.10.cloned.1.call-start = ((), (), s32[]{:S(2)}) async-start(), calls=%async_computation.10 | async-start | bytes 2359296 | tf_op jit(solution)/shard_map/psum | solution.py:188
  936.4 269.5 %reduce-scatter.8.cloned.1.call-start = ((), (), s32[]{:S(2)}) async-start(), calls=%async_computation.14 | async-start | bytes 8912896
  1022.2 1561.2 %reduce-scatter.6.cloned.1.call-start = ((), (), s32[]{:S(2)}) async-start(), calls=%async_computation.12 | async-start | bytes 194641920 | tf_op jit(solution)/shard_map/reduce_scatter | solution.py:268
  1047.4 31.6 copy-start.8
  1086.7 120.6 %copy-start.12 = (bf16[128,2304]{1,0:T(8,128)(2,1)S(1)}, bf16[128,2304]{1,0:T(8,128)(2,1)}, u32[]{:S(2)}) copy-start(bf16[128,2304]{1,0:T(8,128)(2,1)} %copy-done.11) | copy-start | bytes 1769476
  1314.7 1290.3 %all-reduce.12.cloned.1.call-start = ((), (), s32[]{:S(2)}) async-start(), calls=%async_computation.11 | async-start | bytes 1179648 | tf_op jit(solution)/shard_map/psum | solution.py:248
  1324.0 2564.4 %all-reduce.14.cloned.1.call-start = ((), (), s32[]{:S(2)}) async-start(), calls=%async_computation.13 | async-start | bytes 77856768 | tf_op jit(solution)/shard_map/psum | solution.py:271
  2583.5 110.4 %copy-start.6 = (f32[128,2304]{1,0:T(8,128)S(1)}, f32[128,2304]{1,0:T(8,128)}, u32[]{:S(2)}) copy-start(f32[128,2304]{1,0:T(8,128)} %copy-done.5) | copy-start | bytes 3538948
  (37 other events, 191.4 us)
Sparse Core Ops, SparseCore 0:
  9.9 59.7 all-gather.7
  71.5 57.1 all-gather.11
  132.1 75.7 all-gather.9
  209.5 55.6 all-gather.13
  270.4 19.7 all-reduce.5
  292.7 373.4 all-gather.15
  668.2 195.3 all-gather.17
  875.8 19.7 all-reduce.7
  936.5 20.9 all-reduce.9
  1022.4 183.4 reduce-scatter.7
  1314.8 1268.5 reduce-scatter.5
  2586.2 18.8 all-reduce.11
  2607.7 1280.6 all-reduce.13
where the time goes:
time: 3970 us; the launch traced here: 3960 us
  waiting for transfers between devices  3300 us (83%)
  local copies, waits for them, and re-layouts  209 us (5%)
  matrix products  166 us (4%)
  other arithmetic  136 us (3%)
  blocking collectives  127 us (3%)
    reduce_scatter x1, waiting for transfers between devices, on_device(): lax.psum_scatter(jnp.concatenate(columns_list, axis=1), 'fsdp', scatter_d...  1260 us
    psum x1, waiting for transfers between devices, on_device(): summed = lax.psum(summed, 'ctx')  1190 us
    all_gather x1, waiting for transfers between devices, on_device(): lax.all_gather(ffn_in, 'fsdp', axis=0, tiled=True)  373 us
    unnamed x14, waiting for transfers between devices  122 us
    all_gather x1, waiting for transfers between devices, on_device(): lax.all_gather(ffn_out, 'fsdp', axis=0, tiled=True)  121 us
    concatenate x1, other arithmetic, on_device(): jnp.concatenate(columns_list, axis=1)  99.1 us
    psum x1, blocking collectives, on_device(): grad_gains = lax.psum(gain_stack, ('fsdp', 'ctx'))  87.2 us
  transfers between devices with their start and end apart: 13, of which 13 were waited for; matrix products, arithmetic and copies ran while one was open for 5% of the time, Pallas kernels for 0%

commit v1 on v0

--- a/solution.py
+++ b/solution.py
@@ -268,7 +268,7 @@
     summed = lax.psum_scatter(
         jnp.concatenate(columns_list, axis=1), "fsdp", scatter_dimension=0, tiled=True
     )
-    summed = lax.psum(summed, "ctx")
+    summed = jnp.sum(lax.all_gather(summed, "ctx"), axis=0)
     own_width = summed.shape[0]
     edge_two = qcols + 2 * kcols
     edge_three = edge_two + qcols

time: 3970 us -> 5330 us (1.34)
  waiting for transfers between devices: 3300 us -> 4400 us
  blocking collectives: 127 us -> 313 us
  other arithmetic: 136 us -> 219 us
    all_gather x0 -> x1, waiting for transfers between devices: none -> 2290 us  [on_device(): summed = jnp.sum(lax.all_gather(summed, 'ctx'), axis=0)]
    psum x1 -> x0, waiting for transfers between devices: 1190 us -> none  [on_device(): summed = lax.psum(summed, 'ctx')]
    psum x1, blocking collectives: 87.2 us -> 274 us  [on_device(): grad_gains = lax.psum(gain_stack, ('fsdp', 'ctx'))]
    reduce_sum x0 -> x1, other arithmetic: none -> 83.1 us  [on_device(): summed = jnp.sum(lax.all_gather(summed, 'ctx'), axis=0)]
  transfers between devices with their start and end apart: 13 -> 13, of which waited for: 13 -> 13; matrix products, arithmetic and copies ran while one was open for 5% -> 4% of each run, Pallas kernels for 0% -> 0%
where the time goes in v1:
time: 5330 us; the launch traced here: 5320 us
  waiting for transfers between devices  4400 us (83%)
  blocking collectives  313 us (6%)
  other arithmetic  219 us (4%)
  local copies, waits for them, and re-layouts  209 us (4%)
  matrix products  166 us (3%)
    all_gather x1, waiting for transfers between devices, on_device(): summed = jnp.sum(lax.all_gather(summed, 'ctx'), axis=0)  2290 us
    reduce_scatter x1, waiting for transfers between devices, on_device(): lax.psum_scatter(jnp.concatenate(columns_list, axis=1), 'fsdp', scatter_d...  1260 us
    all_gather x1, waiting for transfers between devices, on_device(): lax.all_gather(ffn_in, 'fsdp', axis=0, tiled=True)  373 us
    psum x1, blocking collectives, on_device(): grad_gains = lax.psum(gain_stack, ('fsdp', 'ctx'))  274 us
    unnamed x14, waiting for transfers between devices  122 us
    all_gather x1, waiting for transfers between devices, on_device(): lax.all_gather(ffn_out, 'fsdp', axis=0, tiled=True)  121 us
  transfers between devices with their start and end apart: 13, of which 13 were waited for; matrix products, arithmetic and copies ran while one was open for 4% of the time, Pallas kernels for 0%

profile of v1, /device:TPU:0, one launch (start us, length us, event | category | flops | bytes accessed | tf_op | source)
XLA Modules:
  0.0 5320.1 jit_solution(15417146203641261446)
XLA Ops:
  9.8 59.8 %all-gather.10.cloned.1.call-done = bf16[2304,2,512]{2,1,0:T(2,128)(2,1)} async-done(((bf16[576,2,512]{2,1,0:T(2,128)(2,1)}), bf16[2304,2,512]{2,1,0:T(2,128)(2,1)}) %all-gather.10.cloned.1.call-update) | async-done | bytes 4718608 | tf_op jit(solution)/shard_map/all_gather | solution.py:115
  79.6 39.8 all-gather.1
  132.1 75.8 %all-gather.12.cloned.1.call-done = bf16[2,1024,2,512]{3,2,0,1:T(2,128)(2,1)} async-done(((bf16[2,64,2,512]{3,2,0,1:T(2,128)(2,1)}), bf16[2,1024,2,512]{3,2,0,1:T(2,128)(2,1)}) %all-gather.12.cloned.1.call-update) | async-done | bytes 4194320 | tf_op jit(solution)/shard_map/all_gather | solution.py:128
  244.2 21.1 all-gather.16.cloned.1.call-done
  293.4 372.8 %all-gather.18.cloned.1.call-done = bf16[2304,2,4608]{2,0,1:T(8,128)(2,1)} async-done(((bf16[576,2,4608]{2,0,1:T(8,128)(2,1)}), bf16[2304,2,4608]{2,0,1:T(8,128)(2,1)}) %all-gather.18.cloned.1.call-update) | async-done | bytes 42467344 | tf_op jit(solution)/shard_map/all_gather | solution.py:164
  666.2 51.5 copy.80
  717.8 21.7 fusion
  742.6 121.0 %all-gather.20.cloned.1.call-done = bf16[2304,4608]{1,0:T(8,128)(2,1)} async-done(((bf16[576,4608]{1,0:T(8,128)(2,1)}), bf16[2304,4608]{1,0:T(8,128)(2,1)}) %all-gather.20.cloned.1.call-update) | async-done | bytes 21233680 | tf_op jit(solution)/shard_map/all_gather | solution.py:165
  863.6 12.0 fusion.88
  875.9 19.7 all-reduce.7.cloned.1.call-done
  902.1 12.5 fusion.10
  915.7 20.7 convolution_bitcast_fusion
  938.0 19.6 all-reduce.9.cloned.1.call-done
  1030.7 16.6 fusion.91
  1047.4 31.6 fusion.84
  1086.7 119.2 %reduce-scatter.8.cloned.1.call-done = f32[64,2048]{1,0:T(8,128)} async-done(((f32[1024,2048]{1,0:T(8,128)}), f32[64,2048]{1,0:T(8,128)}) %reduce-scatter.8.cloned.1.call-update) | async-done | bytes 524304
  1215.6 99.1 %pad_maximum_fusion = f32[2304,16896]{1,0:T(8,128)} fusion(f32[2304,4608]{1,0:T(8,128)} %fusion.91, f32[2304,9216]{1,0:T(8,128)} %fusion.84, f32[2304,1024]{1,0:T(8,128)} %fusion.90, f32[2304,2048]{1,0:T(8,128)} %fusion.52), kind=kLoop, calls=%fused_computation | loop fusion | flops 116785152 | bytes 311427072 | tf_op jit(solution)/shard_map/concatenate | solution.py:269
  1324.0 1259.4 %reduce-scatter.6.cloned.1.call-done = f32[576,16896]{1,0:T(8,128)} async-done(((f32[2304,16896]{1,0:T(8,128)}), f32[576,16896]{1,0:T(8,128)}) %reduce-scatter.6.cloned.1.call-update) | async-done | bytes 38928400 | tf_op jit(solution)/shard_map/reduce_scatter | solution.py:268
  2584.2 20.9 all-reduce.11.cloned.1.call-done
  2606.6 273.7 %psum.39 = f32[4,2304]{1,0:T(4,128)} all-reduce(f32[4,2304]{1,0:T(4,128)S(1)} %pad_maximum_fusion.2), channel_id=1, replica_groups=mesh['fsdp'=4,'ctx'=4,'tp'=2] {'fsdp','ctx'}, use_global_device_ids=true, to_apply=%region_20.21 | all-reduce | flops 9216 | bytes 73728 | tf_op jit(solution)/shard_map/psum | solution.py:257
  2882.8 2287.6 %all-gather.22.cloned.1.call-done = f32[2304,16896]{1,0:T(8,128)} async-done(((f32[576,16896]{1,0:T(8,128)}), f32[2304,16896]{1,0:T(8,128)}) %all-gather.22.cloned.1.call-update) | async-done | bytes 155713552 | tf_op jit(solution)/shard_map/all_gather | solution.py:271
  5170.5 83.1 %reduce_sum.182 = f32[576,16896]{1,0:T(8,128)} reduce(f32[4,576,16896]{2,1,0:T(8,128)} %bitcast.43, f32[]{:T(128)} %constant.206.clone.1), dimensions={0}, to_apply=%region_22.23 | reduce | flops 29196288 | bytes 194641920 | tf_op jit(solution)/shard_map/reduce_sum | solution.py:271
  5268.9 14.8 slice.66
  5286.8 26.6 reshape.404
  (208 shorter events, 224.9 us)
Async XLA Ops:
  7.2 62.5 %all-gather.10.cloned.1.call-start = ((), (), s32[]{:S(2)}) async-start(), calls=%async_computation.2 | async-start | bytes 5898240 | tf_op jit(solution)/shard_map/all_gather | solution.py:115
  7.9 120.8 %all-gather.14.cloned.1.call-start = ((), (), s32[]{:S(2)}) async-start(), calls=%async_computation.4 | async-start | bytes 5898240 | tf_op jit(solution)/shard_map/all_gather | solution.py:114
  8.7 199.2 %all-gather.12.cloned.1.call-start = ((), (), s32[]{:S(2)}) async-start(), calls=%async_computation.3 | async-start | bytes 4456448 | tf_op jit(solution)/shard_map/all_gather | solution.py:128
  9.4 110.6 %copy-start.32 = (f32[2304]{0:T(1024)}, f32[2304]{0:T(1024)S(1)}, u32[]{:S(2)}) copy-start(f32[2304]{0:T(1024)S(1)} %get-tuple-element.119) | copy-start | bytes 27652
  9.4 282.3 %copy-start.34 = (f32[2304]{0:T(1024)}, f32[2304]{0:T(1024)S(1)}, u32[]{:S(2)}) copy-start(f32[2304]{0:T(1024)S(1)} %get-tuple-element.118) | copy-start | bytes 27652
  76.5 43.0 copy-start.47
  77.6 187.7 %all-gather.16.cloned.1.call-start = ((), (), s32[]{:S(2)}) async-start(), calls=%async_computation.5 | async-start | bytes 5898240 | tf_op jit(solution)/shard_map/all_gather | solution.py:116
  78.2 212.1 %all-reduce.5.cloned.1.call-start = ((), (), s32[]{:S(2)}) async-start(), calls=%async_computation.6 | async-start | bytes 2359296 | tf_op jit(solution)/shard_map/psum | solution.py:160
  78.3 53.5 %copy-start.41 = (f32[128]{0:T(128)}, f32[128]{0:T(128)S(1)}, u32[]{:S(2)}) copy-start(f32[128]{0:T(128)S(1)} %rsqrt.41) | copy-start | bytes 1540
  120.0 121.7 %copy-start.30 = (pred[2,64,1024]{2,1,0:T(8,128)(4,1)}, pred[2,64,1024]{2,1,0:T(8,128)(4,1)S(1)}, u32[]{:S(2)}) copy-start(pred[2,64,1024]{2,1,0:T(8,128)(4,1)S(1)} %compare_and_fusion) | copy-start | bytes 393220
  132.1 106.9 %copy-start.29 = (bf16[2,64,2,2,256]{4,3,2,1,0:T(2,128)(2,1)}, bf16[2,64,2,2,256]{4,3,2,1,0:T(2,128)(2,1)S(1)}, u32[]{:S(2)}) copy-start(bf16[2,64,2,2,256]{4,3,2,1,0:T(2,128)(2,1)S(1)} %reshape.393) | copy-start | bytes 786436
  244.2 26.1 copy-start.21
  270.3 395.9 %all-gather.18.cloned.1.call-start = ((), (), s32[]{:S(2)}) async-start(), calls=%async_computation.7 | async-start | bytes 53084160 | tf_op jit(solution)/shard_map/all_gather | solution.py:164
  280.6 583.0 %all-gather.20.cloned.1.call-start = ((), (), s32[]{:S(2)}) async-start(), calls=%async_computation.8 | async-start | bytes 26542080 | tf_op jit(solution)/shard_map/all_gather | solution.py:165
  281.4 614.3 %all-reduce.7.cloned.1.call-start = ((), (), s32[]{:S(2)}) async-start(), calls=%async_computation.9 | async-start | bytes 2359296 | tf_op jit(solution)/shard_map/psum | solution.py:173
  291.7 426.0 %copy-start.43 = (f32[128]{0:T(128)}, f32[128]{0:T(128)S(1)}, u32[]{:S(2)}) copy-start(f32[128]{0:T(128)S(1)} %add_rsqrt_fusion.3) | copy-start | bytes 1540
  875.7 81.9 %all-reduce.9.cloned.1.call-start = ((), (), s32[]{:S(2)}) async-start(), calls=%async_computation.10 | async-start | bytes 2359296 | tf_op jit(solution)/shard_map/psum | solution.py:188
  936.4 269.5 %reduce-scatter.8.cloned.1.call-start = ((), (), s32[]{:S(2)}) async-start(), calls=%async_computation.14 | async-start | bytes 8912896
  1022.3 1561.2 %reduce-scatter.6.cloned.1.call-start = ((), (), s32[]{:S(2)}) async-start(), calls=%async_computation.12 | async-start | bytes 194641920 | tf_op jit(solution)/shard_map/reduce_scatter | solution.py:268
  1047.4 31.6 copy-start.8
  1086.7 120.6 %copy-start.12 = (bf16[128,2304]{1,0:T(8,128)(2,1)S(1)}, bf16[128,2304]{1,0:T(8,128)(2,1)}, u32[]{:S(2)}) copy-start(bf16[128,2304]{1,0:T(8,128)(2,1)} %copy-done.11) | copy-start | bytes 1769476
  1314.7 1290.3 %all-reduce.11.cloned.1.call-start = ((), (), s32[]{:S(2)}) async-start(), calls=%async_computation.11 | async-start | bytes 1179648 | tf_op jit(solution)/shard_map/psum | solution.py:248
  1324.0 3846.5 %all-gather.22.cloned.1.call-start = ((), (), s32[]{:S(2)}) async-start(), calls=%async_computation.13 | async-start | bytes 194641920 | tf_op jit(solution)/shard_map/all_gather | solution.py:271
  2583.5 296.9 %copy-start.6 = (f32[128,2304]{1,0:T(8,128)S(1)}, f32[128,2304]{1,0:T(8,128)}, u32[]{:S(2)}) copy-start(f32[128,2304]{1,0:T(8,128)} %copy-done.5) | copy-start | bytes 3538948
  (37 other events, 191.4 us)
Sparse Core Ops, SparseCore 0:
  9.9 59.7 all-gather.9
  71.5 57.1 all-gather.13
  132.1 75.7 all-gather.11
  209.5 55.6 all-gather.15
  270.4 19.7 all-reduce.4
  292.7 373.4 all-gather.17
  668.2 195.3 all-gather.19
  875.8 19.8 all-reduce.6
  936.5 20.9 all-reduce.8
  1022.4 183.4 reduce-scatter.7
  1314.8 1268.5 reduce-scatter.5
  2586.2 18.8 all-reduce.10
  2606.7 2563.6 all-gather.21
